TPU v7x, 512 devices: a whole 4x8x8 slice. The times are simulated.
512 devices in a mesh: dp: 32 (over x, y), table: 16 (over z, core).
Axes of the slice: x: 4, y: 8, z: 8, core: 2. Of those that a mesh axis runs over, the one named last changes fastest.
Arguments:
- table: bfloat16 [12288, 512], P('table'), may hold values from -6 to 6
- history_shard: int32 [512, 256, 1], P(('dp', 'table')), may hold values from 0 to 15; in each aligned block of 256 rows (0 to 255, 256 to 511, ..., all dimensions but the last counted through in order) at most 32 rows name the same one
- history_row: int32 [512, 256], P(('dp', 'table')), may hold values from 0 to 767
- lengths: int32 [512], P(('dp', 'table')), may hold values from 1 to 256, 98304 in all
- w_in: bfloat16 [512, 2048], replicated, may hold values from -0.25 to 0.25
- w_out: bfloat16 [512, 512], replicated, may hold values from -0.25 to 0.25
- cotangent: bfloat16 [512, 256, 512], P(('dp', 'table')), may hold values from -6 to 6
Outputs:
- table_grad: float32 [12288, 512], P('table')
- dense_grad: bfloat16 [512, 512], replicated
Inputs may be any that keep to these rules, and one draw needn't show every extreme that they name: `history_shard`: among the 256 history slots of one device's samples, at most 32 name one table shard, and that bound is met by some shard in some device's slots. `lengths`: some sample has the full length 256.
All inputs are finite; a program needn't handle non-finite values. No bound on the sum of `lengths` on one device may be relied on, other than what follows from the above.
Results may differ from a plain program's by a relative error of at most 0.017.
Values may be sent and summed in bfloat16 or wider, within the bound.
A program may use at most 64 MiB of HBM per device.

v0:
```python
import math
import jax
import jax.numpy as jnp
from jax import lax
from jax.sharding import PartitionSpec as P

HEADS = 4


def layer_norm(values):
    average = jnp.mean(values, axis=-1, keepdims=True)
    centred = values - average
    variance = jnp.mean(centred * centred, axis=-1, keepdims=True)
    return centred * lax.rsqrt(variance + 1e-06)


def hstu_layer(embedded, w_in, w_out, lengths):
    samples_here, seq_span, model_width = embedded.shape
    head_dim = model_width // HEADS
    normed = layer_norm(embedded.astype(jnp.float32)).astype(jnp.bfloat16)
    projected = jax.nn.silu(
        jnp.dot(
            normed.reshape(samples_here * seq_span, model_width),
            w_in,
            preferred_element_type=jnp.float32,
        )
    )
    gate_part = projected[:, :model_width]
    shaped = (samples_here, seq_span, HEADS, head_dim)
    values = projected[:, model_width : 2 * model_width].astype(jnp.bfloat16).reshape(shaped)
    queries = projected[:, 2 * model_width : 3 * model_width].astype(jnp.bfloat16).reshape(shaped)
    keys = projected[:, 3 * model_width :].astype(jnp.bfloat16).reshape(shaped)
    scores = jnp.einsum(
        "blhd,bmhd->bhlm", queries.astype(jnp.float32), keys.astype(jnp.float32)
    ) * head_dim ** (-0.5)
    positions = jnp.arange(seq_span)
    live_keys = (positions[None, None, :] <= positions[None, :, None]) & (
        positions[None, None, :] < lengths[:, None, None]
    )
    weights = (
        jnp.where(live_keys[:, None], jax.nn.silu(scores), 0.0)
        / lengths.astype(jnp.float32)[:, None, None, None]
    )
    weights = weights.astype(jnp.bfloat16)
    attended = jnp.einsum(
        "bhlm,bmhd->blhd", weights.astype(jnp.float32), values.astype(jnp.float32)
    ).reshape(samples_here * seq_span, model_width)
    mixed = (layer_norm(attended) * gate_part).astype(jnp.bfloat16)
    output = jnp.dot(mixed, w_out, preferred_element_type=jnp.float32) + embedded.reshape(
        -1, model_width
    ).astype(jnp.float32)
    return (output, mixed)


def pick_rows(index, length):
    return (index[:, None] == jnp.arange(length, dtype=jnp.int32)[None, :]).astype(jnp.bfloat16)


def per_device(table, history_shard, history_row, lengths, w_in, w_out, cotangent):
    shard_rows, model_width = table.shape
    samples_here, seq_span = history_row.shape
    groups = lax.axis_size("table")
    copies = lax.axis_size("dp")
    slot_count = samples_here * seq_span
    capacity = 2 * slot_count // groups
    owners = history_shard[:, :, 0].reshape(-1)
    local_rows = history_row.reshape(-1)
    owner_hits = (owners[:, None] == jnp.arange(groups)[None, :]).astype(jnp.int32)
    slot_rank = jnp.sum((jnp.cumsum(owner_hits, axis=0) - owner_hits) * owner_hits, axis=1)
    position = owners * capacity + slot_rank
    slot_hits = position[:, None] == jnp.arange(groups * capacity, dtype=jnp.int32)[None, :]
    requested = jnp.sum(jnp.where(slot_hits, local_rows[:, None], 0), axis=0).reshape(
        groups, capacity
    )
    incoming = lax.all_to_all(requested, "table", split_axis=0, concat_axis=0, tiled=True).reshape(
        -1
    )
    reply = jnp.dot(
        pick_rows(incoming, shard_rows), table, preferred_element_type=jnp.float32
    ).astype(jnp.bfloat16)
    received = lax.all_to_all(
        reply.reshape(groups, capacity, model_width),
        "table",
        split_axis=0,
        concat_axis=0,
        tiled=True,
    ).reshape(groups * capacity, model_width)
    place = slot_hits.astype(jnp.bfloat16)
    embedded = jnp.dot(place, received, preferred_element_type=jnp.float32).astype(jnp.bfloat16)
    embedded = embedded.reshape(samples_here, seq_span, model_width)
    output, pullback, mixed = jax.vjp(
        lambda rows_in: hstu_layer(rows_in, w_in, w_out, lengths), embedded, has_aux=True
    )
    row_live = jnp.arange(seq_span)[None, :] < lengths[:, None]
    grad_seed = jnp.where(row_live[:, :, None], cotangent, jnp.zeros_like(cotangent))
    flat_seed = grad_seed.reshape(-1, model_width)
    total_slots = slot_count * copies * groups
    grad_scale = 1.0 / math.sqrt(total_slots)
    dense_part = lax.dot_general(
        mixed, flat_seed, (((0,), (0,)), ((), ())), preferred_element_type=jnp.float32
    ).astype(jnp.bfloat16)
    dense_rows = model_width // groups
    dense_terms = lax.all_to_all(
        dense_part.reshape(groups, dense_rows, model_width),
        "table",
        split_axis=0,
        concat_axis=0,
        tiled=True,
    )
    dense_block = jnp.sum(dense_terms.astype(jnp.float32), axis=0).astype(jnp.bfloat16)
    dense_blocks = lax.all_gather(dense_block, "dp", axis=0, tiled=False)
    dense_sum = jnp.sum(dense_blocks.astype(jnp.float32), axis=0) * grad_scale
    dense_grad = lax.all_gather(dense_sum.astype(jnp.bfloat16), "table", axis=0, tiled=True)
    (row_grad,) = pullback(flat_seed.astype(jnp.float32))
    outgoing = lax.dot_general(
        place,
        row_grad.reshape(-1, model_width),
        (((0,), (0,)), ((), ())),
        preferred_element_type=jnp.float32,
    ).astype(jnp.bfloat16)
    arrived = lax.all_to_all(
        outgoing.reshape(groups, capacity, model_width),
        "table",
        split_axis=0,
        concat_axis=0,
        tiled=True,
    ).reshape(groups * capacity, model_width)
    local_grad = lax.dot_general(
        pick_rows(incoming, shard_rows),
        arrived,
        (((0,), (0,)), ((), ())),
        preferred_element_type=jnp.float32,
    ).astype(jnp.bfloat16)
    part_rows = shard_rows // copies
    terms = lax.all_to_all(
        local_grad.reshape(copies, part_rows, model_width),
        "dp",
        split_axis=0,
        concat_axis=0,
        tiled=True,
    )
    summed = jnp.sum(terms.astype(jnp.float32), axis=0).astype(jnp.bfloat16)
    table_grad = lax.all_gather(summed, "dp", axis=0, tiled=True).astype(jnp.float32)
    return (table_grad, dense_grad)


def solution(mesh):
    in_specs = (
        P("table", None),
        P(("dp", "table"), None, None),
        P(("dp", "table"), None),
        P(("dp", "table")),
        P(),
        P(),
        P(("dp", "table"), None, None),
    )
    out_specs = (P("table", None), P())
    return jax.shard_map(
        per_device, mesh=mesh, in_specs=in_specs, out_specs=out_specs, check_vma=False
    )
```

profile of v0, /device:TPU:1, one launch (start us, length us, event | category | flops | bytes accessed | tf_op | source)
XLA Modules:
  0.0 225.5 jit_solution(14855246301839063184)
XLA Ops:
  11.2 18.6 %all_to_all.29 = s32[16,1,32]{2,1,0:T(1,128)S(1)} all-to-all(s32[16,1,32]{2,1,0:T(1,128)S(1)} %all_to_all.18), channel_id=1, replica_groups=mesh['dp'=32,'table'=16] {'table'}, dimensions={0} | all-to-all | bytes 4096 | tf_op jit(solution)/shard_map/all_to_all | solution.py:75
  31.1 2.5 %fusion.17 = bf16[512,512]{1,0:T(8,128)(2,1)} fusion(bf16[768,512]{1,0:T(8,128)(2,1)} %param.7, s32[512]{0:T(512)S(1)} %eq.68), kind=kOutput, calls=%fused_computation.23 | convolution fusion | flops 403308544 | bytes 1312768 | tf_op jit(solution)/shard_map/dot_general | solution.py:78
  33.6 4.0 %all-to-all-start.1 = ((bf16[16,32,512]{2,1,0:T(8,128)(2,1)}), bf16[16,32,512]{2,1,0:T(8,128)(2,1)S(1)}, u32[]{:S(2)}, u32[]{:S(2)}) async-start(bf16[16,32,512]{2,1,0:T(8,128)(2,1)} %bitcast.6), calls=%async_computation.1 | async-start | bytes 1048576 | tf_op jit(solution)/shard_map/all_to_all | solution.py:81
  38.4 16.6 %all-to-all-done.1 = bf16[16,32,512]{2,1,0:T(8,128)(2,1)S(1)} async-done(((bf16[16,32,512]{2,1,0:T(8,128)(2,1)}), bf16[16,32,512]{2,1,0:T(8,128)(2,1)S(1)}, u32[]{:S(2)}, u32[]{:S(2)}) %all-to-all-start.1) | async-done | bytes 524320 | tf_op jit(solution)/shard_map/all_to_all | solution.py:81
  55.7 2.7 %fusion.70 = (bf16[256,2048]{1,0:T(8,128)(2,1)S(1)}, f32[256,2048]{1,0:T(8,128)}, f32[256,2048]{1,0:T(8,128)}) fusion(bf16[512,2048]{1,0:T(8,128)(2,1)S(1)} %copy-done, f32[256,512]{1,0:T(8,128)S(1)} %get-tuple-element.15, f32[256]{0:T(256)S(1)} %fusion.63, f32[256]{0:T(256)S(1)} %broadcast_multiply_fusion.1), kind=kOutput, calls=%fused_computation.113 | convolution fusion | flops 539885568 | bytes 7866368 | tf_op jit(solution)/shard_map/jvp()/dot_general | solution.py:22
  60.0 1.6 divide_convert_fusion
  62.7 1.2 copy.48
  64.0 1.8 multiply_reduce_fusion.1
  65.9 1.3 convolution_convert_fusion.1
  68.4 1.3 fusion.76
  69.7 2.0 fusion.31
  73.9 1.9 copy.50
  76.6 4.1 %all-to-all-start.4 = ((bf16[16,32,512]{2,1,0:T(8,128)(2,1)}), bf16[16,32,512]{2,1,0:T(8,128)(2,1)}, u32[]{:S(2)}, u32[]{:S(2)}) async-start(bf16[16,32,512]{2,1,0:T(8,128)(2,1)} %bitcast.30), calls=%async_computation.4 | async-start | bytes 1048576 | tf_op jit(solution)/shard_map/all_to_all | solution.py:103
  80.7 2.9 %multiply_reduce_fusion = (f32[256]{0:T(256)S(1)}, f32[256,512]{1,0:T(8,128)S(1)}) fusion(f32[256,512]{1,0:T(8,128)S(1)} %get-tuple-element.15, f32[256]{0:T(256)S(1)} %broadcast_multiply_fusion.1, bf16[512,2048]{1,0:T(8,128)(2,1)S(1)} %copy-done, f32[256,2048]{1,0:T(8,128)} %get-tuple-element.16, f32[256,512]{1,0:T(8,128)} %get-tuple-element.8, ...), kind=kOutput, calls=%fused_computation.56 | convolution fusion | flops 545390336 | bytes 6555648 | tf_op jit(solution)/shard_map/transpose(jvp())/dot_general | solution.py:22
  84.0 1.3 convolution_convert_fusion.2
  85.3 11.7 %all-to-all-done.4 = bf16[16,32,512]{2,1,0:T(8,128)(2,1)} async-done(((bf16[16,32,512]{2,1,0:T(8,128)(2,1)}), bf16[16,32,512]{2,1,0:T(8,128)(2,1)}, u32[]{:S(2)}, u32[]{:S(2)}) %all-to-all-start.4) | async-done | bytes 524320 | tf_op jit(solution)/shard_map/all_to_all | solution.py:103
  96.9 3.5 %all-to-all-start.2 = ((bf16[16,32,512]{2,1,0:T(8,128)(2,1)}), bf16[16,32,512]{2,1,0:T(8,128)(2,1)S(1)}, u32[]{:S(2)}, u32[]{:S(2)}) async-start(bf16[16,32,512]{2,1,0:T(8,128)(2,1)} %bitcast.27), calls=%async_computation.2 | async-start | bytes 1048576 | tf_op jit(solution)/shard_map/all_to_all | solution.py:121
  100.5 1.7 reduce_sum.150
  102.2 14.9 %all-to-all-done.2 = bf16[16,32,512]{2,1,0:T(8,128)(2,1)S(1)} async-done(((bf16[16,32,512]{2,1,0:T(8,128)(2,1)}), bf16[16,32,512]{2,1,0:T(8,128)(2,1)S(1)}, u32[]{:S(2)}, u32[]{:S(2)}) %all-to-all-start.2) | async-done | bytes 524320 | tf_op jit(solution)/shard_map/all_to_all | solution.py:121
  117.8 31.6 %all_to_all.30 = bf16[32,24,512]{2,1,0:T(8,128)(2,1)S(1)} all-to-all(bf16[32,24,512]{2,1,0:T(8,128)(2,1)S(1)} %bitcast.113), channel_id=1, replica_groups=mesh['dp'=32,'table'=16] {'dp'}, dimensions={0} | all-to-all | bytes 1572864 | tf_op jit(solution)/shard_map/all_to_all | solution.py:135
  149.5 40.4 %all_gather.12 = bf16[768,512]{1,0:T(8,128)(2,1)S(1)} all-gather(bf16[24,512]{1,0:T(8,128)(2,1)S(1)} %reduce_sum.149), channel_id=1, replica_groups=mesh['dp'=32,'table'=16] {'dp'}, dimensions={0}, use_global_device_ids=true | all-gather | bytes 811008 | tf_op jit(solution)/shard_map/all_gather | solution.py:143
  189.9 1.4 convert_element_type.164
  191.3 1.4 convert_reduce_fusion
  192.7 25.2 %all_gather.15 = bf16[512,512]{1,0:T(8,128)(2,1)S(1)} all-gather(bf16[32,512]{1,0:T(8,128)(2,1)S(1)} %multiply_convert_fusion.4), channel_id=1, replica_groups=mesh['dp'=32,'table'=16] {'table'}, dimensions={0}, use_global_device_ids=true | all-gather | bytes 557056 | tf_op jit(solution)/shard_map/all_gather | solution.py:113
  (65 shorter events, 15.0 us)
Async XLA Ops:
  7.2 48.5 %copy-start = (bf16[512,2048]{1,0:T(8,128)(2,1)S(1)}, bf16[512,2048]{1,0:T(8,128)(2,1)}, u32[]{:S(2)}) copy-start(bf16[512,2048]{1,0:T(8,128)(2,1)} %param.11) | copy-start | bytes 6291460
  33.6 21.4 %all-to-all-start.1 = ((bf16[16,32,512]{2,1,0:T(8,128)(2,1)}), bf16[16,32,512]{2,1,0:T(8,128)(2,1)S(1)}, u32[]{:S(2)}, u32[]{:S(2)}) async-start(bf16[16,32,512]{2,1,0:T(8,128)(2,1)} %bitcast.6), calls=%async_computation.1 | async-start | bytes 1048576 | tf_op jit(solution)/shard_map/all_to_all | solution.py:81
  59.3 0.7 copy-start.5
  59.4 2.1 copy-start.7
  60.0 1.6 copy-start.9
  61.6 0.8 copy-start.3
  61.6 2.4 %copy-start.2 = (bf16[1,256,512]{2,1,0:T(8,128)(2,1)S(1)}, bf16[1,256,512]{2,1,0:T(8,128)(2,1)}, u32[]{:S(2)}) copy-start(bf16[1,256,512]{2,1,0:T(8,128)(2,1)} %param.13) | copy-start | bytes 786436
  61.9 0.8 copy-start.1
  64.0 1.9 copy-start.4
  69.7 2.1 copy-start.6
  69.7 2.4 %copy-start.8 = (bf16[256,512]{0,1:T(8,128)(2,1)S(1)}, bf16[256,512]{0,1:T(8,128)(2,1)}, u32[]{:S(2)}) copy-start(bf16[256,512]{0,1:T(8,128)(2,1)} %copy-done.7) | copy-start | bytes 786436
  73.9 6.9 %copy-start.10 = (bf16[256,512]{1,0:T(8,128)(2,1)S(1)}, bf16[256,512]{1,0:T(8,128)(2,1)}, u32[]{:S(2)}) copy-start(bf16[256,512]{1,0:T(8,128)(2,1)} %copy.52) | copy-start | bytes 786436
  76.6 20.3 %all-to-all-start.4 = ((bf16[16,32,512]{2,1,0:T(8,128)(2,1)}), bf16[16,32,512]{2,1,0:T(8,128)(2,1)}, u32[]{:S(2)}, u32[]{:S(2)}) async-start(bf16[16,32,512]{2,1,0:T(8,128)(2,1)} %bitcast.30), calls=%async_computation.4 | async-start | bytes 1048576 | tf_op jit(solution)/shard_map/all_to_all | solution.py:103
  96.9 20.2 %all-to-all-start.2 = ((bf16[16,32,512]{2,1,0:T(8,128)(2,1)}), bf16[16,32,512]{2,1,0:T(8,128)(2,1)S(1)}, u32[]{:S(2)}, u32[]{:S(2)}) async-start(bf16[16,32,512]{2,1,0:T(8,128)(2,1)} %bitcast.27), calls=%async_computation.2 | async-start | bytes 1048576 | tf_op jit(solution)/shard_map/all_to_all | solution.py:121
  100.4 90.9 %all-gather.3.cloned.1.call-start = ((), (), s32[]{:S(2)}) async-start(), calls=%async_computation.5 | async-start | bytes 1081344 | tf_op jit(solution)/shard_map/all_gather | solution.py:111
Sparse Core Ops, SparseCore 0:
  104.4 79.3 all-gather.2
where the time goes:
time: 226 us
  blocking collectives  116 us (51%)
  waiting for transfers between devices  43.2 us (19%)
  matrix products  20.1 us (9%)
  between operations  14.9 us (7%)
  starting transfers between devices  11.7 us (5%)
  other arithmetic  10.8 us (5%)
  local copies, waits for them, and re-layouts  8.98 us (4%)
    all_gather x1, blocking collectives, per_device(): lax.all_gather(summed, 'dp', axis=0, tiled=True).astype(jnp.float32)  40.4 us
    all_to_all x1, blocking collectives, per_device(): lax.all_to_all(local_grad.reshape(copies, part_rows, model_width), 'dp',...  31.6 us
    all_gather x1, blocking collectives, per_device(): lax.all_gather(dense_sum.astype(jnp.bfloat16), 'table', axis=0, tiled=True)  25.2 us
    all_to_all x1, blocking collectives, per_device(): lax.all_to_all(requested, 'table', split_axis=0, concat_axis=0, tiled=True)  18.6 us
    all_to_all x1, waiting for transfers between devices, per_device(): lax.all_to_all(reply.reshape(groups, capacity, model_width), 'table', spl...  16.6 us
    all_to_all x1, waiting for transfers between devices, per_device(): lax.all_to_all(outgoing.reshape(groups, capacity, model_width), 'table',...  14.9 us
    all_to_all x1, waiting for transfers between devices, per_device(): lax.all_to_all(dense_part.reshape(groups, dense_rows, model_width), 'tabl...  11.7 us
    dot_general x2, matrix products, hstu_layer(): jnp.dot(normed.reshape(samples_here * seq_span, model_width), w_in, prefe...  5.66 us
  transfers between devices with their start and end apart: 4, of which 3 were waited for; matrix products, arithmetic and copies ran while one was open for 4% of the time, Pallas kernels for 0%

commit v1 on v0

--- a/solution.py
+++ b/solution.py
@@ -110,7 +110,9 @@
     dense_block = jnp.sum(dense_terms.astype(jnp.float32), axis=0).astype(jnp.bfloat16)
     dense_blocks = lax.all_gather(dense_block, "dp", axis=0, tiled=False)
     dense_sum = jnp.sum(dense_blocks.astype(jnp.float32), axis=0) * grad_scale
-    dense_grad = lax.all_gather(dense_sum.astype(jnp.bfloat16), "table", axis=0, tiled=True)
+    part = dense_sum.astype(jnp.bfloat16)
+    sent = jnp.stack([part] * lax.axis_size("table"))
+    dense_grad = jnp.concatenate(lax.all_to_all(sent, "table", 0, 0), axis=0)
     (row_grad,) = pullback(flat_seed.astype(jnp.float32))
     outgoing = lax.dot_general(
         place,

time: 226 us -> 256 us (1.13)
  the two profiles are of different devices: /device:TPU:1 before, /device:TPU:64 now
where the time goes in v1:
time: 256 us; the launch traced here: 255 us
  waiting for transfers between devices  99.9 us (39%)
  blocking collectives  64.2 us (25%)
  starting transfers between devices  34.4 us (13%)
  matrix products  21 us (8%)
  between operations  14.9 us (6%)
  other arithmetic  10.8 us (4%)
  local copies, waits for them, and re-layouts  9.82 us (4%)
    all_gather x1, waiting for transfers between devices, per_device(): dense_blocks = lax.all_gather(dense_block, 'dp', axis=0, tiled=False)  63.6 us
    all_gather x1, blocking collectives, per_device(): lax.all_gather(summed, 'dp', axis=0, tiled=True).astype(jnp.float32)  48.3 us
    all_to_all x1, blocking collectives, per_device(): lax.all_to_all(requested, 'table', split_axis=0, concat_axis=0, tiled=True)  16 us
    all_to_all x1, waiting for transfers between devices, per_device(): lax.all_to_all(reply.reshape(groups, capacity, model_width), 'table', spl...  13.6 us
    all_to_all x1, waiting for transfers between devices, per_device(): lax.all_to_all(outgoing.reshape(groups, capacity, model_width), 'table',...  12.8 us
    all_to_all x1, starting transfers between devices, per_device(): lax.all_to_all(local_grad.reshape(copies, part_rows, model_width), 'dp',...  9.96 us
    all_to_all x1, waiting for transfers between devices, per_device(): lax.all_to_all(dense_part.reshape(groups, dense_rows, model_width), 'tabl...  9.9 us
    all_to_all x1, starting transfers between devices, per_device(): dense_grad = jnp.concatenate(lax.all_to_all(sent, 'table', 0, 0), axis=0)  7.77 us
  transfers between devices with their start and end apart: 6, of which 4 were waited for; matrix products, arithmetic and copies ran while one was open for 4% of the time, Pallas kernels for 0%

profile of v1, /device:TPU:64, one launch (start us, length us, event | category | flops | bytes accessed | tf_op | source)
XLA Modules:
  0.0 255.1 jit_solution(9165055078764034867)
XLA Ops:
  11.2 16.0 %all_to_all.34 = s32[16,1,32]{2,1,0:T(1,128)S(1)} all-to-all(s32[16,1,32]{2,1,0:T(1,128)S(1)} %all_to_all.21), channel_id=1, replica_groups=mesh['dp'=32,'table'=16] {'table'}, dimensions={0} | all-to-all | bytes 4096 | tf_op jit(solution)/shard_map/all_to_all | solution.py:75
  28.4 2.5 fusion.17
  31.0 4.8 %all-to-all-start.1 = ((bf16[16,32,512]{2,1,0:T(8,128)(2,1)}), bf16[16,32,512]{2,1,0:T(8,128)(2,1)S(1)}, u32[]{:S(2)}, u32[]{:S(2)}) async-start(bf16[16,32,512]{2,1,0:T(8,128)(2,1)} %bitcast.6), calls=%async_computation.1 | async-start | bytes 1048576 | tf_op jit(solution)/shard_map/all_to_all | solution.py:81
  36.5 13.6 %all-to-all-done.1 = bf16[16,32,512]{2,1,0:T(8,128)(2,1)S(1)} async-done(((bf16[16,32,512]{2,1,0:T(8,128)(2,1)}), bf16[16,32,512]{2,1,0:T(8,128)(2,1)S(1)}, u32[]{:S(2)}, u32[]{:S(2)}) %all-to-all-start.1) | async-done | bytes 524320 | tf_op jit(solution)/shard_map/all_to_all | solution.py:81
  50.8 2.7 %fusion.70 = (bf16[256,2048]{1,0:T(8,128)(2,1)S(1)}, f32[256,2048]{1,0:T(8,128)}, f32[256,2048]{1,0:T(8,128)}) fusion(bf16[512,2048]{1,0:T(8,128)(2,1)S(1)} %copy-done, f32[256,512]{1,0:T(8,128)S(1)} %get-tuple-element.15, f32[256]{0:T(256)S(1)} %fusion.63, f32[256]{0:T(256)S(1)} %broadcast_multiply_fusion.1), kind=kOutput, calls=%fused_computation.113 | convolution fusion | flops 539885568 | bytes 7866368 | tf_op jit(solution)/shard_map/jvp()/dot_general | solution.py:22
  55.2 1.6 divide_convert_fusion
  59.2 1.8 multiply_reduce_fusion.1
  63.6 1.3 fusion.76
  64.9 2.0 fusion.31
  69.0 1.9 copy.50
  71.7 5.9 %all-to-all-start.4 = ((bf16[16,32,512]{2,1,0:T(8,128)(2,1)}), bf16[16,32,512]{2,1,0:T(8,128)(2,1)}, u32[]{:S(2)}, u32[]{:S(2)}) async-start(bf16[16,32,512]{2,1,0:T(8,128)(2,1)} %bitcast.30), calls=%async_computation.4 | async-start | bytes 1048576 | tf_op jit(solution)/shard_map/all_to_all | solution.py:103
  77.7 2.9 %multiply_reduce_fusion = (f32[256]{0:T(256)S(1)}, f32[256,512]{1,0:T(8,128)S(1)}) fusion(f32[256,512]{1,0:T(8,128)S(1)} %get-tuple-element.15, f32[256]{0:T(256)S(1)} %broadcast_multiply_fusion.1, bf16[512,2048]{1,0:T(8,128)(2,1)S(1)} %copy-done, f32[256,2048]{1,0:T(8,128)} %get-tuple-element.16, f32[256,512]{1,0:T(8,128)} %get-tuple-element.8, ...), kind=kOutput, calls=%fused_computation.56 | convolution fusion | flops 545390336 | bytes 6555648 | tf_op jit(solution)/shard_map/transpose(jvp())/dot_general | solution.py:22
  80.9 1.3 convolution_convert_fusion.2
  82.2 9.9 %all-to-all-done.4 = bf16[16,32,512]{2,1,0:T(8,128)(2,1)} async-done(((bf16[16,32,512]{2,1,0:T(8,128)(2,1)}), bf16[16,32,512]{2,1,0:T(8,128)(2,1)}, u32[]{:S(2)}, u32[]{:S(2)}) %all-to-all-start.4) | async-done | bytes 524320 | tf_op jit(solution)/shard_map/all_to_all | solution.py:103
  92.1 5.9 %all-to-all-start.2 = ((bf16[16,32,512]{2,1,0:T(8,128)(2,1)}), bf16[16,32,512]{2,1,0:T(8,128)(2,1)S(1)}, u32[]{:S(2)}, u32[]{:S(2)}) async-start(bf16[16,32,512]{2,1,0:T(8,128)(2,1)} %bitcast.27), calls=%async_computation.2 | async-start | bytes 1048576 | tf_op jit(solution)/shard_map/all_to_all | solution.py:123
  98.0 1.7 reduce_sum.150
  99.8 12.8 %all-to-all-done.2 = bf16[16,32,512]{2,1,0:T(8,128)(2,1)S(1)} async-done(((bf16[16,32,512]{2,1,0:T(8,128)(2,1)}), bf16[16,32,512]{2,1,0:T(8,128)(2,1)S(1)}, u32[]{:S(2)}, u32[]{:S(2)}) %all-to-all-start.2) | async-done | bytes 524320 | tf_op jit(solution)/shard_map/all_to_all | solution.py:123
  112.6 1.6 fusion.16
  114.1 10.0 %all-to-all-start.3 = ((bf16[32,24,512]{2,1,0:T(8,128)(2,1)}), bf16[32,24,512]{2,1,0:T(8,128)(2,1)S(1)}, u32[]{:S(2)}, u32[]{:S(2)}) async-start(bf16[32,24,512]{2,1,0:T(8,128)(2,1)} %bitcast.115), calls=%async_computation.3 | async-start | bytes 1572864 | tf_op jit(solution)/shard_map/all_to_all | solution.py:137
  124.1 63.6 %all-gather.3.cloned.1.call-done = bf16[1024,512]{1,0:T(8,128)(2,1)} async-done(((bf16[32,512]{1,0:T(8,128)(2,1)}), bf16[1024,512]{1,0:T(8,128)(2,1)}) %all-gather.3.cloned.1.call-update) | async-done | bytes 1048592 | tf_op jit(solution)/shard_map/all_gather | solution.py:111
  187.7 1.4 convert_reduce_fusion
  190.0 7.8 %all-to-all-start.5 = ((bf16[16,32,512]{2,1,0:T(8,128)(2,1)}), bf16[16,32,512]{2,1,0:T(8,128)(2,1)S(1)}, u32[]{:S(2)}, u32[]{:S(2)}) async-start(bf16[16,32,512]{2,1,0:T(8,128)(2,1)} %stack.2), calls=%async_computation.5 | async-start | bytes 1048576 | tf_op jit(solution)/shard_map/all_to_all | solution.py:115
  197.8 48.3 %all_gather.9 = bf16[768,512]{1,0:T(8,128)(2,1)S(1)} all-gather(bf16[24,512]{1,0:T(8,128)(2,1)S(1)} %reduce_sum.149), channel_id=1, replica_groups=mesh['dp'=32,'table'=16] {'dp'}, dimensions={0}, use_global_device_ids=true | all-gather | bytes 811008 | tf_op jit(solution)/shard_map/all_gather | solution.py:145
  246.1 1.4 convert_element_type.166
  (68 shorter events, 17.6 us)
Async XLA Ops:
  7.2 43.6 %copy-start = (bf16[512,2048]{1,0:T(8,128)(2,1)S(1)}, bf16[512,2048]{1,0:T(8,128)(2,1)}, u32[]{:S(2)}) copy-start(bf16[512,2048]{1,0:T(8,128)(2,1)} %param.11) | copy-start | bytes 6291460
  31.0 19.2 %all-to-all-start.1 = ((bf16[16,32,512]{2,1,0:T(8,128)(2,1)}), bf16[16,32,512]{2,1,0:T(8,128)(2,1)S(1)}, u32[]{:S(2)}, u32[]{:S(2)}) async-start(bf16[16,32,512]{2,1,0:T(8,128)(2,1)} %bitcast.6), calls=%async_computation.1 | async-start | bytes 1048576 | tf_op jit(solution)/shard_map/all_to_all | solution.py:81
  54.4 0.7 copy-start.5
  54.6 2.1 copy-start.7
  55.2 1.6 copy-start.9
  56.7 0.8 copy-start.3
  56.7 2.4 copy-start.2
  57.1 0.8 copy-start.1
  59.1 1.9 copy-start.4
  64.9 2.1 copy-start.6
  64.9 2.4 copy-start.8
  69.0 8.6 %copy-start.10 = (bf16[256,512]{1,0:T(8,128)(2,1)S(1)}, bf16[256,512]{1,0:T(8,128)(2,1)}, u32[]{:S(2)}) copy-start(bf16[256,512]{1,0:T(8,128)(2,1)} %copy.52) | copy-start | bytes 786436
  71.7 20.3 %all-to-all-start.4 = ((bf16[16,32,512]{2,1,0:T(8,128)(2,1)}), bf16[16,32,512]{2,1,0:T(8,128)(2,1)}, u32[]{:S(2)}, u32[]{:S(2)}) async-start(bf16[16,32,512]{2,1,0:T(8,128)(2,1)} %bitcast.30), calls=%async_computation.4 | async-start | bytes 1048576 | tf_op jit(solution)/shard_map/all_to_all | solution.py:103
  92.1 20.5 %all-to-all-start.2 = ((bf16[16,32,512]{2,1,0:T(8,128)(2,1)}), bf16[16,32,512]{2,1,0:T(8,128)(2,1)S(1)}, u32[]{:S(2)}, u32[]{:S(2)}) async-start(bf16[16,32,512]{2,1,0:T(8,128)(2,1)} %bitcast.27), calls=%async_computation.2 | async-start | bytes 1048576 | tf_op jit(solution)/shard_map/all_to_all | solution.py:123
  98.0 89.7 %all-gather.3.cloned.1.call-start = ((), (), s32[]{:S(2)}) async-start(), calls=%async_computation.6 | async-start | bytes 1081344 | tf_op jit(solution)/shard_map/all_gather | solution.py:111
  114.1 75.0 %all-to-all-start.3 = ((bf16[32,24,512]{2,1,0:T(8,128)(2,1)}), bf16[32,24,512]{2,1,0:T(8,128)(2,1)S(1)}, u32[]{:S(2)}, u32[]{:S(2)}) async-start(bf16[32,24,512]{2,1,0:T(8,128)(2,1)} %bitcast.115), calls=%async_computation.3 | async-start | bytes 1572864 | tf_op jit(solution)/shard_map/all_to_all | solution.py:137
  190.0 57.5 %all-to-all-start.5 = ((bf16[16,32,512]{2,1,0:T(8,128)(2,1)}), bf16[16,32,512]{2,1,0:T(8,128)(2,1)S(1)}, u32[]{:S(2)}, u32[]{:S(2)}) async-start(bf16[16,32,512]{2,1,0:T(8,128)(2,1)} %stack.2), calls=%async_computation.5 | async-start | bytes 1048576 | tf_op jit(solution)/shard_map/all_to_all | solution.py:115
Sparse Core Ops, SparseCore 0:
  102.0 85.6 all-gather.2
